TPU v7x, 256 devices: a whole 4x4x8 slice. The times are simulated.
256 devices in a mesh: dp: 32 (over y, z), head: 8 (over x, core).
Axes of the slice: x: 4, y: 4, z: 8, core: 2. Of those that a mesh axis runs over, the one named last changes fastest.
Arguments:
- queries: bfloat16 [32768, 4096], P('dp', 'head'), may hold values from -6 to 6
- keys: bfloat16 [32768, 4096], P('dp', 'head'), may hold values from -6 to 6
- values: bfloat16 [32768, 4096], P('dp', 'head'), may hold values from -100 to 100
- out_grad: bfloat16 [32768, 4096], P('dp', 'head'), may hold values from -6 to 6
- norm_gain: float32 [4096], P('head'), may hold values from 0.1 to 1.9
- decay_table: float32 [16, 8], P('head'), may hold values from 0 to 0.52, as said below
- decay_index: int32 [16, 32768], P('head', 'dp'), may hold values from 0 to 7
- rollout_lengths: int32 [6], replicated, may hold values from 1 to 16384, 32768 in all
- move_partner: int32 [32], replicated, may hold values from 0 to 31, as said below
- move_slot: int32 [32], replicated, may hold values from 0 to 31, as said below
Outputs:
- query_grad: bfloat16 [32768, 4096], P('dp', 'head')
- key_grad: bfloat16 [32768, 4096], P('dp', 'head')
- value_grad: bfloat16 [32768, 4096], P('dp', 'head')
Inputs may be any that keep to these rules, and one draw needn't show every extreme that they name: `decay_table`: positive rates. `rollout_lengths`: they sum to 32768. move_partner[d] is either d itself or a row whose index differs from d in exactly one bit, and the partner of the partner is the row itself. `move_slot`: one block of each row.
All inputs are finite; a program needn't handle non-finite values.
Results may differ from a plain program's by a relative error of at most 0.0063.
Values may be sent and summed in bfloat16 or wider, within the bound.
No kernel may reach another device: no remote copies, remote signals or barrier semaphores. Data moves between devices by JAX's collectives and lax.ppermute only.
A program may use at most 128 MiB of HBM per device.

v0:
```python
import jax
import jax.numpy as jnp
from jax import lax
from jax.sharding import PartitionSpec as P

HEAD_DIM = 256
BLOCK_LEN = 32
FEATURES = 4096
EPSILON = 1e-05


def entering(part, axis, combine, identity, reverse):
    count = lax.axis_size(axis)
    place = lax.axis_index(axis)
    ahead = count - 1 - place if reverse else place
    gathered = jax.tree.map(lambda a: lax.all_gather(a, axis), part)
    state = jax.tree.map(lambda a, e: jnp.zeros_like(a) + jnp.asarray(e, a.dtype), part, identity)

    def one(turn, state):
        source = count - 1 - turn if reverse else turn
        return combine(
            state, jax.tree.map(lambda a: lax.dynamic_index_in_dim(a, source, 0, False), gathered)
        )

    return lax.fori_loop(0, ahead, one, state)


def edge_factors(rate, flag):
    segment = jnp.cumsum(flag.astype(jnp.int32))
    total = jnp.cumsum(rate, axis=1)
    first = jnp.where(segment[None, :] == 0, jnp.exp(-total), 0.0)
    last = jnp.where(segment[None, :] == segment[-1], jnp.exp(total - total[:, -1:]), 0.0)
    whole = jnp.where(segment[-1] == 0, jnp.exp(-total[:, -1]), 0.0)
    return (total, segment, first, last, whole)


def decay_matrix(total_row, segment):
    count = segment.shape[0]
    places = jnp.arange(count)
    inside = (segment[:, None] == segment[None, :]) & (places[:, None] >= places[None, :])
    return jnp.where(
        inside, jnp.exp(jnp.minimum(total_row[None, :] - total_row[:, None], 0.0)), 0.0
    )


def combine_states(before, behind):
    return (before[0] * behind[0], behind[0][:, None, None] * before[1] + behind[1])


def take_block(array, block_id, length, axis_dim):
    return lax.dynamic_slice_in_dim(array, block_id * length, length, axis_dim)


def place_block(array, block, block_id, axis_dim):
    return lax.dynamic_update_slice_in_dim(array, block, block_id * block.shape[axis_dim], axis_dim)


def contract_first(left, right):
    return lax.dot_general(
        left, right, (((0,), (0,)), ((), ())), preferred_element_type=jnp.float32
    )


def contract_last(left, right):
    return lax.dot_general(
        left, right, (((1,), (1,)), ((), ())), preferred_element_type=jnp.float32
    )


def local(
    queries,
    keys,
    values,
    out_grad,
    norm_gain,
    decay_table,
    decay_index,
    rollout_lengths,
    move_partner,
    move_slot,
):
    row_index = lax.axis_index("dp")
    row_tokens = queries.shape[0]
    heads_here = decay_table.shape[0]
    length = BLOCK_LEN
    partner = move_partner[row_index]
    own_slot = move_slot[row_index]
    outgoing = (
        take_block(queries, own_slot, length, 0),
        take_block(keys, own_slot, length, 0),
        take_block(values, own_slot, length, 0),
        take_block(out_grad, own_slot, length, 0),
        take_block(decay_index, own_slot, length, 1),
    )
    arrived = (
        lax.all_gather(outgoing[0], "dp", axis=0, tiled=True),
        lax.all_gather(outgoing[1], "dp", axis=0, tiled=True),
        lax.all_gather(outgoing[2], "dp", axis=0, tiled=True),
        lax.all_gather(outgoing[3], "dp", axis=0, tiled=True),
        lax.all_gather(outgoing[4], "dp", axis=1, tiled=True),
    )
    guest = tuple(
        (
            take_block(member, partner, length, axis_dim)
            for member, axis_dim in zip(arrived, (0, 0, 0, 0, 1))
        )
    )
    packed_q = place_block(queries, guest[0], own_slot, 0)
    packed_k = place_block(keys, guest[1], own_slot, 0)
    packed_v = place_block(values, guest[2], own_slot, 0)
    packed_dy = place_block(out_grad, guest[3], own_slot, 0)
    packed_index = place_block(decay_index, guest[4], own_slot, 1)
    level_ids = jnp.arange(decay_table.shape[1], dtype=jnp.int32)
    rate = jnp.sum(
        jnp.where(packed_index[:, :, None] == level_ids, decay_table[:, None, :], 0.0), axis=2
    )
    starts = jnp.cumsum(rollout_lengths) - rollout_lengths
    position = row_index * row_tokens + jnp.arange(row_tokens, dtype=jnp.int32)
    flag = jnp.any(position[:, None] == starts[None, :], axis=1)
    total, segment, first, last, whole = edge_factors(rate, flag)
    head_cols = []
    local_states = []
    for head_pos in range(heads_here):
        columns = slice(head_pos * HEAD_DIM, (head_pos + 1) * HEAD_DIM)
        head_cols.append(columns)
        gated_values = (packed_v[:, columns].astype(jnp.float32) * last[head_pos][:, None]).astype(
            jnp.bfloat16
        )
        local_states.append(contract_first(packed_k[:, columns], gated_values))
    stacked = jnp.stack(local_states)
    identity = (jnp.ones_like(whole), jnp.zeros_like(stacked))
    _, carry_in = entering((whole, stacked), "dp", combine_states, identity, False)
    carry_half = carry_in.astype(jnp.bfloat16)
    decays = []
    weight_list = []
    retained_parts = []
    for head_pos in range(heads_here):
        columns = head_cols[head_pos]
        query_head = packed_q[:, columns]
        decay = decay_matrix(total[head_pos], segment)
        scores = contract_last(query_head, packed_k[:, columns])
        weights = (scores * decay / HEAD_DIM).astype(jnp.bfloat16)
        inner_part = jnp.dot(weights, packed_v[:, columns], preferred_element_type=jnp.float32)
        cross_part = (
            first[head_pos][:, None]
            * jnp.dot(query_head, carry_half[head_pos], preferred_element_type=jnp.float32)
            / HEAD_DIM
        )
        decays.append(decay)
        weight_list.append(weights)
        retained_parts.append(inner_part + cross_part)
    retained = jnp.concatenate(retained_parts, axis=1)
    scaled = norm_gain * packed_dy.astype(jnp.float32)
    squares, inner = lax.psum(
        (jnp.sum(retained * retained, axis=1), jnp.sum(scaled * retained, axis=1)), "head"
    )
    recip = lax.rsqrt(squares / FEATURES + EPSILON)
    norm_grad = (
        recip[:, None] * scaled - (recip**3 * inner / FEATURES)[:, None] * retained
    ).astype(jnp.bfloat16)
    back_locals = []
    for head_pos in range(heads_here):
        columns = head_cols[head_pos]
        weighted = (norm_grad[:, columns].astype(jnp.float32) * first[head_pos][:, None]).astype(
            jnp.bfloat16
        )
        back_locals.append(contract_first(packed_q[:, columns], weighted) / HEAD_DIM)
    back_stack = jnp.stack(back_locals)
    _, carry_back = entering(
        (whole, back_stack),
        "dp",
        combine_states,
        (jnp.ones_like(whole), jnp.zeros_like(back_stack)),
        True,
    )
    back_half = carry_back.astype(jnp.bfloat16)
    query_parts = []
    key_parts = []
    value_parts = []
    for head_pos in range(heads_here):
        columns = head_cols[head_pos]
        query_head = packed_q[:, columns]
        key_head = packed_k[:, columns]
        value_head = packed_v[:, columns]
        grad_head = norm_grad[:, columns]
        grad_scores = contract_last(grad_head, value_head)
        grad_weights = (grad_scores * decays[head_pos] / HEAD_DIM).astype(jnp.bfloat16)
        query_part = jnp.dot(grad_weights, key_head, preferred_element_type=jnp.float32)
        query_part = (
            query_part
            + first[head_pos][:, None] * contract_last(grad_head, carry_half[head_pos]) / HEAD_DIM
        )
        key_part = contract_first(grad_weights, query_head)
        key_part = key_part + last[head_pos][:, None] * contract_last(
            value_head, back_half[head_pos]
        )
        value_part = contract_first(weight_list[head_pos], grad_head)
        value_part = value_part + last[head_pos][:, None] * jnp.dot(
            key_head, back_half[head_pos], preferred_element_type=jnp.float32
        )
        query_parts.append(query_part)
        key_parts.append(key_part)
        value_parts.append(value_part)
    packed_grads = (
        jnp.concatenate(query_parts, axis=1).astype(jnp.bfloat16),
        jnp.concatenate(key_parts, axis=1).astype(jnp.bfloat16),
        jnp.concatenate(value_parts, axis=1).astype(jnp.bfloat16),
    )
    leaving = tuple((take_block(member, own_slot, length, 0) for member in packed_grads))
    returned_all = (
        lax.all_gather(leaving[0], "dp", axis=0, tiled=True),
        lax.all_gather(leaving[1], "dp", axis=0, tiled=True),
        lax.all_gather(leaving[2], "dp", axis=0, tiled=True),
    )
    returned = tuple((take_block(member, partner, length, 0) for member in returned_all))
    query_grad = place_block(packed_grads[0], returned[0], own_slot, 0)
    key_grad = place_block(packed_grads[1], returned[1], own_slot, 0)
    value_grad = place_block(packed_grads[2], returned[2], own_slot, 0)
    return (query_grad, key_grad, value_grad)


def solution(mesh):
    placed = (
        P("dp", "head"),
        P("dp", "head"),
        P("dp", "head"),
        P("dp", "head"),
        P("head"),
        P("head", None),
        P("head", "dp"),
        P(),
        P(),
        P(),
    )
    return jax.shard_map(
        local,
        mesh=mesh,
        in_specs=placed,
        out_specs=(P("dp", "head"), P("dp", "head"), P("dp", "head")),
        check_vma=False,
    )
```

profile of v0, /device:TPU:2, one launch (start us, length us, event | category | flops | bytes accessed | tf_op | source)
XLA Modules:
  0.0 900.6 jit_solution(8727087491861123065)
XLA Ops:
  19.7 46.3 %all-gather.3 = s32[32,32,2]{1,2,0:T(2,128)S(1)} all-gather(s32[1,32,2]{1,2,0:T(2,128)S(1)} %fusion.70), channel_id=1, replica_groups=mesh['dp'=32,'head'=8] {'dp'}, dimensions={0}, use_global_device_ids=true | all-gather | bytes 8448 | tf_op jit(solution)/shard_map/all_gather | solution.py:100
  68.4 23.5 %all-gather.18.cloned.1.call-done = bf16[1024,512]{1,0:T(8,128)(2,1)} async-done(((bf16[32,512]{1,0:T(8,128)(2,1)}), bf16[1024,512]{1,0:T(8,128)(2,1)}) %all-gather.18.cloned.1.call-update) | async-done | bytes 1048592 | tf_op jit(solution)/shard_map/all_gather | solution.py:98
  93.7 74.8 %all-gather.16.cloned.1.call-done = bf16[1024,512]{1,0:T(8,128)(2,1)} async-done(((bf16[32,512]{1,0:T(8,128)(2,1)}), bf16[1024,512]{1,0:T(8,128)(2,1)}) %all-gather.16.cloned.1.call-update) | async-done | bytes 1048592 | tf_op jit(solution)/shard_map/all_gather | solution.py:97
  174.4 72.2 %all-reduce = f32[64]{0:T(128)S(1)} all-reduce(f32[64]{0:T(128)S(1)} %fusion.73), channel_id=2, replica_groups=mesh['dp'=32,'head'=8] {'dp'}, use_global_device_ids=true, to_apply=%add | all-reduce | flops 64 | bytes 512
  248.6 73.8 %all-gather.14.cloned.1.call-done = bf16[1024,512]{1,0:T(8,128)(2,1)} async-done(((bf16[32,512]{1,0:T(8,128)(2,1)}), bf16[1024,512]{1,0:T(8,128)(2,1)}) %all-gather.14.cloned.1.call-update) | async-done | bytes 1048592 | tf_op jit(solution)/shard_map/all_gather | solution.py:96
  323.2 2.1 multiply_convert_fusion.2
  327.1 2.1 multiply_convert_fusion.3
  332.3 129.7 %all-gather.28.cloned.1.call-done = f32[64,256,256]{2,1,0:T(8,128)} async-done(((f32[2,256,256]{2,1,0:T(8,128)}), f32[64,256,256]{2,1,0:T(8,128)}) %all-gather.28.cloned.1.call-update) | async-done | bytes 16777232 | tf_op jit(solution)/shard_map/all_gather | solution.py:16
  466.7 11.1 %all-reduce.1 = (f32[1024]{0:T(1024)S(1)}, f32[1024]{0:T(1024)S(1)}) all-reduce(f32[1024]{0:T(1024)S(1)} %get-tuple-element.146, f32[1024]{0:T(1024)S(1)} %get-tuple-element.145), channel_id=1, replica_groups=mesh['dp'=32,'head'=8] {'head'}, use_global_device_ids=true, to_apply=%region_12.13 | all-reduce | flops 2048 | bytes 16384 | tf_op jit(solution)/shard_map/psum | solution.py:154
  477.8 2.0 subtract_convert_fusion
  483.8 2.3 multiply_convert_fusion
  488.1 2.2 multiply_convert_fusion.1
  493.4 3.3 fusion.32
  496.7 3.3 fusion.27
  500.0 157.3 %all-gather.30.cloned.1.call-done = f32[64,256,256]{2,1,0:T(8,128)} async-done(((f32[2,256,256]{2,1,0:T(8,128)}), f32[64,256,256]{2,1,0:T(8,128)}) %all-gather.30.cloned.1.call-update) | async-done | bytes 16777232 | tf_op jit(solution)/shard_map/all_gather | solution.py:16
  657.3 38.7 %while.27 = (s32[]{:T(128)}, f32[2,256,256]{2,1,0:T(8,128)S(1)}, s32[]{:T(128)}, f32[32,2]{1,0:T(8,128)S(1)}, f32[32,2,256,256]{3,2,1,0:T(8,128)}, /*index=5*/s32[]{:T(128)}, s32[]{:T(128)}, s32[]{:T(128)}, s32[]{:T(128)}) while((s32[]{:T(128)}, f32[2,256,256]{2,1,0:T(8,128)S(1)}, s32[]{:T(128)}, f32[32,2]{1,0:T(8,128)S(1)}, ...), condition=%wide.region_14.15_spmd, body=%wide.region_13.14_spmd.sunk | while | flops 262150 | bytes 1573043 | solution.py:25
  699.0 2.6 fusion.35
  704.9 28.5 %all-gather.22.cloned.1.call-done = bf16[1024,512]{1,0:T(8,128)(2,1)} async-done(((bf16[32,512]{1,0:T(8,128)(2,1)}), bf16[1024,512]{1,0:T(8,128)(2,1)}) %all-gather.22.cloned.1.call-update) | async-done | bytes 1048592 | tf_op jit(solution)/shard_map/all_gather | solution.py:211
  734.3 2.2 dynamic_update_slice.31
  736.5 2.3 copy.57
  739.9 70.0 %all-gather.26.cloned.1.call-done = bf16[1024,512]{1,0:T(8,128)(2,1)} async-done(((bf16[32,512]{1,0:T(8,128)(2,1)}), bf16[1024,512]{1,0:T(8,128)(2,1)}) %all-gather.26.cloned.1.call-update) | async-done | bytes 1048592 | tf_op jit(solution)/shard_map/all_gather | solution.py:213
  809.9 76.5 %all-gather.24.cloned.1.call-done = bf16[1024,512]{1,0:T(8,128)(2,1)} async-done(((bf16[32,512]{1,0:T(8,128)(2,1)}), bf16[1024,512]{1,0:T(8,128)(2,1)}) %all-gather.24.cloned.1.call-update) | async-done | bytes 1048592 | tf_op jit(solution)/shard_map/all_gather | solution.py:212
  887.3 2.2 dynamic_update_slice.33
  889.4 2.3 copy.59
  (227 shorter events, 90.2 us)
Async XLA Ops:
  7.2 59.2 %copy-start.20 = (f32[2,8]{1,0:T(2,128)S(1)}, f32[2,8]{1,0:T(2,128)}, u32[]{:S(2)}) copy-start(f32[2,8]{1,0:T(2,128)} %param.19) | copy-start | bytes 196
  7.2 2.5 copy-start.18
  7.2 10.9 %copy-start.23 = (s32[6]{0:T(128)S(1)}, s32[6]{0:T(128)}, u32[]{:S(2)}) copy-start(s32[6]{0:T(128)} %param.21) | copy-start | bytes 76
  7.2 8.1 copy-start.22
  7.2 84.7 %all-gather.18.cloned.1.call-start = ((), (), s32[]{:S(2)}) async-start(), calls=%async_computation.2 | async-start | bytes 1081344 | tf_op jit(solution)/shard_map/all_gather | solution.py:98
  12.4 156.1 %all-gather.16.cloned.1.call-start = ((), (), s32[]{:S(2)}) async-start(), calls=%async_computation.1 | async-start | bytes 1081344 | tf_op jit(solution)/shard_map/all_gather | solution.py:97
  13.1 233.6 %all-gather.20.cloned.1.call-start = ((), (), s32[]{:S(2)}) async-start(), calls=%async_computation.3 | async-start | bytes 1081344 | tf_op jit(solution)/shard_map/all_gather | solution.py:99
  14.6 307.8 %all-gather.14.cloned.1.call-start = ((), (), s32[]{:S(2)}) async-start(), calls=%async_computation | async-start | bytes 1081344 | tf_op jit(solution)/shard_map/all_gather | solution.py:96
  15.3 446.7 %all-gather.28.cloned.1.call-start = ((), (), s32[]{:S(2)}) async-start(), calls=%async_computation.7 | async-start | bytes 17301504 | tf_op jit(solution)/shard_map/all_gather | solution.py:16
  18.1 154.9 %copy-start.24 = (u32[256]{0:T(256)S(1)}, u32[256]{0:T(256)}, u32[]{:S(2)}) copy-start(u32[256]{0:T(256)} %constant.107) | copy-start | bytes 3076
  93.7 77.2 %copy-start.6 = (bf16[1024,512]{0,1:T(8,128)(2,1)}, bf16[1024,512]{0,1:T(8,128)(2,1)S(1)}, u32[]{:S(2)}) copy-start(bf16[1024,512]{0,1:T(8,128)(2,1)S(1)} %dynamic_update_slice.29) | copy-start | bytes 3145732
  170.8 486.5 %all-gather.30.cloned.1.call-start = ((), (), s32[]{:S(2)}) async-start(), calls=%async_computation.8 | async-start | bytes 17301504 | tf_op jit(solution)/shard_map/all_gather | solution.py:16
  323.2 3.9 copy-start.4
  325.3 3.9 copy-start.12
  462.0 3.7 copy-start.19
  479.8 4.0 copy-start.8
  483.6 249.9 %all-gather.22.cloned.1.call-start = ((), (), s32[]{:S(2)}) async-start(), calls=%async_computation.4 | async-start | bytes 1081344 | tf_op jit(solution)/shard_map/all_gather | solution.py:211
  486.1 4.2 copy-start.14
  500.0 309.9 %all-gather.26.cloned.1.call-start = ((), (), s32[]{:S(2)}) async-start(), calls=%async_computation.6 | async-start | bytes 1081344 | tf_op jit(solution)/shard_map/all_gather | solution.py:213
  657.3 38.8 %copy-start.11 = (f32[1024,256]{0,1:T(8,128)S(1)}, f32[1024,256]{0,1:T(8,128)}, u32[]{:S(2)}) copy-start(f32[1024,256]{0,1:T(8,128)} %fusion.27) | copy-start | bytes 3145732
  698.1 3.5 copy-start.5
  698.9 187.4 %all-gather.24.cloned.1.call-start = ((), (), s32[]{:S(2)}) async-start(), calls=%async_computation.5 | async-start | bytes 1081344 | tf_op jit(solution)/shard_map/all_gather | solution.py:212
  699.0 2.6 copy-start.16
  699.0 3.4 copy-start.10
  (10 other events, 16.4 us)
Sparse Core Ops, SparseCore 0:
  12.5 79.3 all-gather.17
  94.5 73.9 all-gather.15
  171.6 73.8 all-gather.19
  248.5 73.8 all-gather.13
  324.8 137.1 all-gather.27
  483.7 173.5 all-gather.29
  659.9 73.4 all-gather.21
  736.0 73.8 all-gather.25
  812.5 73.8 all-gather.23
where the time goes:
time: 903 us; the launch traced here: 901 us
  waiting for transfers between devices  634 us (70%)
  blocking collectives  130 us (14%)
  other arithmetic  46.7 us (5%)
  local copies, waits for them, and re-layouts  37.5 us (4%)
  matrix products  34 us (4%)
  between operations  17.1 us (2%)
    all_gather x2, waiting for transfers between devices, entering(): gathered = jax.tree.map(lambda a: lax.all_gather(a, axis), part)  287 us
    all_gather x1, waiting for transfers between devices, local(): lax.all_gather(leaving[1], 'dp', axis=0, tiled=True)  76.5 us
    all_gather x1, waiting for transfers between devices, local(): lax.all_gather(outgoing[1], 'dp', axis=0, tiled=True)  74.8 us
    all_gather x1, waiting for transfers between devices, local(): lax.all_gather(outgoing[0], 'dp', axis=0, tiled=True)  73.8 us
    unnamed x1, blocking collectives  72.2 us
    all_gather x1, waiting for transfers between devices, local(): lax.all_gather(leaving[2], 'dp', axis=0, tiled=True)  70 us
    all_gather x1, blocking collectives, local(): lax.all_gather(outgoing[4], 'dp', axis=1, tiled=True)  46.3 us
    add x31, other arithmetic, combine_states(): behind[0][:, None, None] * before[1] + behind[1]  37.5 us
  transfers between devices with their start and end apart: 9, of which 8 were waited for; matrix products, arithmetic and copies ran while one was open for 10% of the time, Pallas kernels for 0%

commit v1 on v0

--- a/solution.py
+++ b/solution.py
@@ -93,7 +93,9 @@
         take_block(decay_index, own_slot, length, 1),
     )
     arrived = (
-        lax.all_gather(outgoing[0], "dp", axis=0, tiled=True),
+        jnp.concatenate(
+            lax.all_to_all(jnp.stack([outgoing[0]] * lax.axis_size("dp")), "dp", 0, 0), axis=0
+        ),
         lax.all_gather(outgoing[1], "dp", axis=0, tiled=True),
         lax.all_gather(outgoing[2], "dp", axis=0, tiled=True),
         lax.all_gather(outgoing[3], "dp", axis=0, tiled=True),

time: 903 us -> 829 us (0.918)
  waiting for transfers between devices: 634 us -> 541 us
  blocking collectives: 130 us -> 141 us
    all_gather x1 -> x0, waiting for transfers between devices: 73.8 us -> none  [local(): lax.all_gather(outgoing[0], 'dp', axis=0, tiled=True)]
    all_gather x2, waiting for transfers between devices: 287 us -> 266 us  [entering(): gathered = jax.tree.map(lambda a: lax.all_gather(a, axis), part)]
    unnamed x1, blocking collectives: 72.2 us -> 83.3 us
  transfers between devices with their start and end apart: 9 -> 9, of which waited for: 8 -> 7; matrix products, arithmetic and copies ran while one was open for 10% -> 11% of each run, Pallas kernels for 0% -> 0%
where the time goes in v1:
time: 829 us; the launch traced here: 826 us
  waiting for transfers between devices  541 us (65%)
  blocking collectives  141 us (17%)
  other arithmetic  46.7 us (6%)
  local copies, waits for them, and re-layouts  38.6 us (5%)
  matrix products  34 us (4%)
  between operations  17.3 us (2%)
    all_gather x2, waiting for transfers between devices, entering(): gathered = jax.tree.map(lambda a: lax.all_gather(a, axis), part)  266 us
    unnamed x1, blocking collectives  83.3 us
    all_gather x1, waiting for transfers between devices, local(): lax.all_gather(leaving[1], 'dp', axis=0, tiled=True)  76.5 us
    all_gather x1, waiting for transfers between devices, local(): lax.all_gather(outgoing[1], 'dp', axis=0, tiled=True)  75.3 us
    all_gather x1, waiting for transfers between devices, local(): lax.all_gather(leaving[2], 'dp', axis=0, tiled=True)  70 us
    all_gather x1, blocking collectives, local(): lax.all_gather(outgoing[4], 'dp', axis=1, tiled=True)  46.3 us
    add x31, other arithmetic, combine_states(): behind[0][:, None, None] * before[1] + behind[1]  37.5 us
    all_gather x1, waiting for transfers between devices, local(): lax.all_gather(leaving[0], 'dp', axis=0, tiled=True)  28.4 us
  transfers between devices with their start and end apart: 9, of which 7 were waited for; matrix products, arithmetic and copies ran while one was open for 11% of the time, Pallas kernels for 0%

profile of v1, /device:TPU:2, one launch (start us, length us, event | category | flops | bytes accessed | tf_op | source)
XLA Modules:
  0.0 825.8 jit_solution(2661427984109557643)
XLA Ops:
  19.5 46.3 %all-gather.3 = s32[32,32,2]{1,2,0:T(2,128)S(1)} all-gather(s32[1,32,2]{1,2,0:T(2,128)S(1)} %fusion.70), channel_id=1, replica_groups=mesh['dp'=32,'head'=8] {'dp'}, dimensions={0}, use_global_device_ids=true | all-gather | bytes 8448 | tf_op jit(solution)/shard_map/all_gather | solution.py:102
  68.2 24.2 %all-gather.15.cloned.1.call-done = bf16[1024,512]{1,0:T(8,128)(2,1)} async-done(((bf16[32,512]{1,0:T(8,128)(2,1)}), bf16[1024,512]{1,0:T(8,128)(2,1)}) %all-gather.15.cloned.1.call-update) | async-done | bytes 1048592 | tf_op jit(solution)/shard_map/all_gather | solution.py:100
  94.3 75.3 %all-gather.13.cloned.1.call-done = bf16[1024,512]{1,0:T(8,128)(2,1)} async-done(((bf16[32,512]{1,0:T(8,128)(2,1)}), bf16[1024,512]{1,0:T(8,128)(2,1)}) %all-gather.13.cloned.1.call-update) | async-done | bytes 1048592 | tf_op jit(solution)/shard_map/all_gather | solution.py:99
  173.1 6.1 all-to-all-start
  182.7 83.3 %all-reduce = f32[64]{0:T(128)S(1)} all-reduce(f32[64]{0:T(128)S(1)} %fusion.73), channel_id=2, replica_groups=mesh['dp'=32,'head'=8] {'dp'}, use_global_device_ids=true, to_apply=%add | all-reduce | flops 64 | bytes 512
  268.8 2.1 multiply_convert_fusion.2
  272.7 2.1 multiply_convert_fusion.3
  278.0 108.8 %all-gather.25.cloned.1.call-done = f32[64,256,256]{2,1,0:T(8,128)} async-done(((f32[2,256,256]{2,1,0:T(8,128)}), f32[64,256,256]{2,1,0:T(8,128)}) %all-gather.25.cloned.1.call-update) | async-done | bytes 16777232 | tf_op jit(solution)/shard_map/all_gather | solution.py:16
  391.5 11.1 %all-reduce.1 = (f32[1024]{0:T(1024)S(1)}, f32[1024]{0:T(1024)S(1)}) all-reduce(f32[1024]{0:T(1024)S(1)} %get-tuple-element.146, f32[1024]{0:T(1024)S(1)} %get-tuple-element.145), channel_id=1, replica_groups=mesh['dp'=32,'head'=8] {'head'}, use_global_device_ids=true, to_apply=%region_12.13 | all-reduce | flops 2048 | bytes 16384 | tf_op jit(solution)/shard_map/psum | solution.py:156
  402.6 2.0 subtract_convert_fusion
  408.6 2.3 multiply_convert_fusion
  412.8 2.2 multiply_convert_fusion.1
  418.1 3.3 fusion.32
  421.4 3.3 fusion.27
  424.7 157.6 %all-gather.27.cloned.1.call-done = f32[64,256,256]{2,1,0:T(8,128)} async-done(((f32[2,256,256]{2,1,0:T(8,128)}), f32[64,256,256]{2,1,0:T(8,128)}) %all-gather.27.cloned.1.call-update) | async-done | bytes 16777232 | tf_op jit(solution)/shard_map/all_gather | solution.py:16
  582.4 38.7 %while.27 = (s32[]{:T(128)}, f32[2,256,256]{2,1,0:T(8,128)S(1)}, s32[]{:T(128)}, f32[32,2]{1,0:T(8,128)S(1)}, f32[32,2,256,256]{3,2,1,0:T(8,128)}, /*index=5*/s32[]{:T(128)}, s32[]{:T(128)}, s32[]{:T(128)}, s32[]{:T(128)}) while((s32[]{:T(128)}, f32[2,256,256]{2,1,0:T(8,128)S(1)}, s32[]{:T(128)}, f32[32,2]{1,0:T(8,128)S(1)}, ...), condition=%wide.region_14.15_spmd, body=%wide.region_13.14_spmd.sunk | while | flops 262150 | bytes 1573043 | solution.py:25
  624.1 2.6 fusion.35
  630.0 28.4 %all-gather.19.cloned.1.call-done = bf16[1024,512]{1,0:T(8,128)(2,1)} async-done(((bf16[32,512]{1,0:T(8,128)(2,1)}), bf16[1024,512]{1,0:T(8,128)(2,1)}) %all-gather.19.cloned.1.call-update) | async-done | bytes 1048592 | tf_op jit(solution)/shard_map/all_gather | solution.py:213
  659.2 2.2 dynamic_update_slice.31
  661.4 2.3 copy.57
  664.8 70.0 %all-gather.23.cloned.1.call-done = bf16[1024,512]{1,0:T(8,128)(2,1)} async-done(((bf16[32,512]{1,0:T(8,128)(2,1)}), bf16[1024,512]{1,0:T(8,128)(2,1)}) %all-gather.23.cloned.1.call-update) | async-done | bytes 1048592 | tf_op jit(solution)/shard_map/all_gather | solution.py:215
  734.8 76.5 %all-gather.21.cloned.1.call-done = bf16[1024,512]{1,0:T(8,128)(2,1)} async-done(((bf16[32,512]{1,0:T(8,128)(2,1)}), bf16[1024,512]{1,0:T(8,128)(2,1)}) %all-gather.21.cloned.1.call-update) | async-done | bytes 1048592 | tf_op jit(solution)/shard_map/all_gather | solution.py:214
  812.2 2.2 dynamic_update_slice.33
  814.3 2.3 copy.59
  (225 shorter events, 91.2 us)
Async XLA Ops:
  7.2 59.0 %copy-start.19 = (f32[2,8]{1,0:T(2,128)S(1)}, f32[2,8]{1,0:T(2,128)}, u32[]{:S(2)}) copy-start(f32[2,8]{1,0:T(2,128)} %param.19) | copy-start | bytes 196
  7.2 10.8 %copy-start.22 = (s32[6]{0:T(128)S(1)}, s32[6]{0:T(128)}, u32[]{:S(2)}) copy-start(s32[6]{0:T(128)} %param.21) | copy-start | bytes 76
  7.2 8.1 copy-start.21
  7.2 3.2 copy-start.20
  7.2 85.3 %all-gather.15.cloned.1.call-start = ((), (), s32[]{:S(2)}) async-start(), calls=%async_computation.2 | async-start | bytes 1081344 | tf_op jit(solution)/shard_map/all_gather | solution.py:100
  13.0 156.6 %all-gather.13.cloned.1.call-start = ((), (), s32[]{:S(2)}) async-start(), calls=%async_computation.1 | async-start | bytes 1081344 | tf_op jit(solution)/shard_map/all_gather | solution.py:99
  13.8 252.4 %all-gather.17.cloned.1.call-start = ((), (), s32[]{:S(2)}) async-start(), calls=%async_computation.3 | async-start | bytes 1081344 | tf_op jit(solution)/shard_map/all_gather | solution.py:101
  15.3 371.4 %all-gather.25.cloned.1.call-start = ((), (), s32[]{:S(2)}) async-start(), calls=%async_computation.7 | async-start | bytes 17301504 | tf_op jit(solution)/shard_map/all_gather | solution.py:16
  94.3 78.8 %copy-start.6 = (bf16[1024,512]{0,1:T(8,128)(2,1)}, bf16[1024,512]{0,1:T(8,128)(2,1)S(1)}, u32[]{:S(2)}) copy-start(bf16[1024,512]{0,1:T(8,128)(2,1)S(1)} %dynamic_update_slice.29) | copy-start | bytes 3145732
  170.7 10.7 %copy-start.23 = (u32[256]{0:T(256)S(1)}, u32[256]{0:T(256)}, u32[]{:S(2)}) copy-start(u32[256]{0:T(256)} %constant.107) | copy-start | bytes 3076
  173.1 95.0 %all-to-all-start = ((bf16[32,32,512]{2,1,0:T(8,128)(2,1)}), bf16[32,32,512]{2,1,0:T(8,128)(2,1)}, u32[]{:S(2)}, u32[]{:S(2)}) async-start(bf16[32,32,512]{2,1,0:T(8,128)(2,1)} %stack.14), calls=%async_computation | async-start | bytes 2097152 | tf_op jit(solution)/shard_map/all_to_all | solution.py:97
  179.2 403.2 %all-gather.27.cloned.1.call-start = ((), (), s32[]{:S(2)}) async-start(), calls=%async_computation.8 | async-start | bytes 17301504 | tf_op jit(solution)/shard_map/all_gather | solution.py:16
  268.8 3.9 copy-start.4
  271.0 3.9 copy-start.12
  386.8 3.7 copy-start.18
  404.5 4.0 copy-start.8
  408.3 250.0 %all-gather.19.cloned.1.call-start = ((), (), s32[]{:S(2)}) async-start(), calls=%async_computation.4 | async-start | bytes 1081344 | tf_op jit(solution)/shard_map/all_gather | solution.py:213
  410.8 4.2 copy-start.14
  424.7 310.1 %all-gather.23.cloned.1.call-start = ((), (), s32[]{:S(2)}) async-start(), calls=%async_computation.6 | async-start | bytes 1081344 | tf_op jit(solution)/shard_map/all_gather | solution.py:215
  582.4 38.8 %copy-start.11 = (f32[1024,256]{0,1:T(8,128)S(1)}, f32[1024,256]{0,1:T(8,128)}, u32[]{:S(2)}) copy-start(f32[1024,256]{0,1:T(8,128)} %fusion.27) | copy-start | bytes 3145732
  623.1 3.5 copy-start.5
  624.0 187.3 %all-gather.21.cloned.1.call-start = ((), (), s32[]{:S(2)}) async-start(), calls=%async_computation.5 | async-start | bytes 1081344 | tf_op jit(solution)/shard_map/all_gather | solution.py:214
  624.0 2.6 copy-start.16
  624.0 3.4 copy-start.10
  (9 other events, 13.8 us)
Sparse Core Ops, SparseCore 0:
  13.2 79.2 all-gather.14
  95.6 73.9 all-gather.12
  172.8 74.2 all-gather.16
  249.5 137.1 all-gather.24
  408.4 173.8 all-gather.26
  584.8 73.5 all-gather.18
  660.9 73.8 all-gather.22
  737.4 73.8 all-gather.20
